TPU v7x, 128 devices: a whole 4x4x4 slice. The times are simulated.
128 devices in a mesh: dp: 2 (over core), expert: 64 (over y, x, z).
Axes of the slice: x: 4, y: 4, z: 4, core: 2. Of those that a mesh axis runs over, the one named last changes fastest.
Arguments:
- tokens: bfloat16 [16384, 2048], P(('dp', 'expert')), may hold values from -6 to 6
- cotangent: bfloat16 [16384, 2048], P(('dp', 'expert')), may hold values from -6 to 6
- routes: int32 [16384, 2], P(('dp', 'expert')), may hold values from 0 to 15, all different within a row; in each aligned block of 128 rows (0 to 127, 128 to 255, ...) at most 24 rows name the same one
- gates: float32 [16384, 2], P(('dp', 'expert')), may hold values from 0.1 to 1
- capacity: int32 [16], replicated, may hold values from 13 to 24, as said below
- layout: int32 [64], replicated, may hold values from 0 to 63, each once
- partner: int32 [64], replicated, may hold values from 0 to 63, as said below
- w_in: float32 [64, 2048, 256], P('expert'), may hold values from -0.125 to 0.125
- w_out: float32 [64, 256, 2048], P('expert'), may hold values from -0.1875 to 0.1875
- m_in: bfloat16 [64, 2048, 256], P('expert'), may hold values from -5 to 5
- v_in: bfloat16 [64, 2048, 256], P('expert'), may hold values from 0.099609375 to 4
- m_out: bfloat16 [64, 256, 2048], P('expert'), may hold values from -5 to 5
- v_out: bfloat16 [64, 256, 2048], P('expert'), may hold values from 0.099609375 to 4
Outputs:
- mixed: bfloat16 [16384, 2048], P(('dp', 'expert'))
- token_grad: bfloat16 [16384, 2048], P(('dp', 'expert'))
- new_w_in: float32 [64, 2048, 256], P('expert')
- new_w_out: float32 [64, 256, 2048], P('expert')
- new_m_in: bfloat16 [64, 2048, 256], P('expert')
- new_v_in: bfloat16 [64, 2048, 256], P('expert')
- new_m_out: bfloat16 [64, 256, 2048], P('expert')
- new_v_out: bfloat16 [64, 256, 2048], P('expert')
Inputs may be any that keep to these rules, and one draw needn't show every extreme that they name: `routes`: in the rows of one device no expert is named by more than 24 pairs, a bound that some block reaches; each token names 2 different experts. `capacity`: some expert has exactly 24 and some other exactly that minimum. `layout`: A permutation. partner[d] is d or the index half the expert axis away, and partner[partner[d]] = d; both kinds occur.
All inputs are finite; a program needn't handle non-finite values.
Results may differ from a plain program's by a relative error of at most 0.0079.
Values may be sent and summed in bfloat16 or wider, within the bound.
A program may use at most 128 MiB of HBM per device.

v0:
```python
import jax
import jax.numpy as jnp
from jax import lax
from jax.sharding import PartitionSpec as P

GROUP = 4


def relay(block, step):
    ndp = lax.axis_size("dp")
    nexp = lax.axis_size("expert")
    route = []
    for d in range(ndp):
        sign = 1 if d % 2 == 0 else -1
        for e in range(nexp):
            route.append((d * nexp + e, d * nexp + (e + sign * step) % nexp))
    return lax.ppermute(block, ("dp", "expert"), route)


def migrate(blocks):
    ndp = lax.axis_size("dp")
    step = lax.axis_size("expert") // 4
    here = lax.axis_index("dp")
    halves = tuple(
        (
            lax.dynamic_slice_in_dim(b, here * (b.shape[0] // ndp), b.shape[0] // ndp, 0)
            for b in blocks
        )
    )
    moved = relay(relay(halves, step), step)
    return tuple((lax.all_gather(m, "dp", axis=0, tiled=True) for m in moved))


def gelu_tanh(value):
    return jax.nn.gelu(value, approximate=True)


def adamw(weight, first, second, grad):
    first_f = 0.9 * first.astype(jnp.float32) + 0.1 * grad
    second_f = 0.999 * second.astype(jnp.float32) + 0.001 * grad * grad
    corrected = first_f / (1.0 - 0.9**10) / (jnp.sqrt(second_f / (1.0 - 0.999**10)) + 1e-08)
    updated = weight - 0.01 * (corrected + 0.1 * weight)
    return (updated, first_f.astype(jnp.bfloat16), second_f.astype(jnp.bfloat16))


def local(
    tokens,
    cotangent,
    routes,
    gates,
    capacity,
    layout,
    partner,
    w_in,
    w_out,
    m_in,
    v_in,
    m_out,
    v_out,
):
    width = tokens.shape[1]
    count = tokens.shape[0]
    topk = routes.shape[1]
    experts = capacity.shape[0]
    slots = 3 * count * topk // (2 * experts)
    nexp = lax.axis_size("expert")
    here = lax.axis_index("expert")
    moved = jnp.take(partner, here) != here
    flat_routes = routes.reshape(-1)
    onehot = (flat_routes[:, None] == jnp.arange(experts, dtype=jnp.int32)[None, :]).astype(
        jnp.int32
    )
    position = jnp.sum((jnp.cumsum(onehot, 0) - 1) * onehot, 1)
    limit = jnp.sum(onehot * capacity[None, :], 1)
    slot = jnp.where(position < limit, flat_routes * slots + position, experts * slots)
    x_rows = jnp.repeat(tokens, topk, axis=0)
    scaled = (
        gates.reshape(-1)[:, None] * jnp.repeat(cotangent, topk, axis=0).astype(jnp.float32)
    ).astype(jnp.bfloat16)

    def build(rows):
        filled = jnp.zeros((experts * slots + 1, width), jnp.bfloat16).at[slot].set(rows)
        return filled[:-1].reshape(experts, slots, width)

    x_buf = build(x_rows)
    g_buf = build(scaled)
    weight_in, weight_out = (w_in[0], w_out[0])
    first_in, second_in, first_out, second_out = (m_in[0], v_in[0], m_out[0], v_out[0])
    held = jnp.take(layout, partner, axis=0)
    other = migrate(
        (
            weight_in.astype(jnp.bfloat16),
            weight_out.astype(jnp.bfloat16),
            first_in,
            second_in,
            first_out,
            second_out,
        )
    )
    other_w = (other[0].astype(weight_in.dtype), other[1].astype(weight_out.dtype))
    other_m = other[2:]
    weight_in = jnp.where(moved, other_w[0], weight_in)
    weight_out = jnp.where(moved, other_w[1], weight_out)
    first_in = jnp.where(moved, other_m[0], first_in)
    second_in = jnp.where(moved, other_m[1], second_in)
    first_out = jnp.where(moved, other_m[2], first_out)
    second_out = jnp.where(moved, other_m[3], second_out)
    target_expert = held // GROUP
    send_x = jnp.take(x_buf, target_expert, axis=0)
    send_g = jnp.take(g_buf, target_expert, axis=0)
    recv_x, recv_g = (
        lax.all_to_all(send_x, "expert", split_axis=0, concat_axis=0, tiled=True),
        lax.all_to_all(send_g, "expert", split_axis=0, concat_axis=0, tiled=True),
    )
    rows = recv_x.reshape(-1, width)
    grows = recv_g.reshape(-1, width)
    wb_in = weight_in.astype(jnp.bfloat16)
    wb_out = weight_out.astype(jnp.bfloat16)
    pre = jnp.dot(rows, wb_in, preferred_element_type=jnp.float32)
    hidden, pull = jax.vjp(gelu_tanh, pre)
    hidden = hidden.astype(jnp.bfloat16)
    part = jnp.dot(hidden, wb_out, preferred_element_type=jnp.float32).astype(jnp.bfloat16)
    dhid = lax.dot_general(
        grows, wb_out, (((1,), (1,)), ((), ())), preferred_element_type=jnp.float32
    )
    dpre = pull(dhid)[0].astype(jnp.bfloat16)
    xpart = lax.dot_general(
        dpre, wb_in, (((1,), (1,)), ((), ())), preferred_element_type=jnp.float32
    ).astype(jnp.bfloat16)
    grad_in = lax.dot_general(
        rows, dpre, (((0,), (0,)), ((), ())), preferred_element_type=jnp.float32
    )
    grad_out = lax.dot_general(
        hidden, grows, (((0,), (0,)), ((), ())), preferred_element_type=jnp.float32
    )
    back_part, back_dx = (
        lax.all_to_all(
            part.reshape(nexp, slots, width), "expert", split_axis=0, concat_axis=0, tiled=True
        ),
        lax.all_to_all(
            xpart.reshape(nexp, slots, width), "expert", split_axis=0, concat_axis=0, tiled=True
        ),
    )
    grad_in, grad_out = lax.psum((grad_in, grad_out), "dp")
    new_w_in, new_m_in, new_v_in = adamw(weight_in, first_in, second_in, grad_in)
    new_w_out, new_m_out, new_v_out = adamw(weight_out, first_out, second_out, grad_out)
    owners = (target_expert[:, None] == jnp.arange(experts, dtype=jnp.int32)[None, :]).astype(
        jnp.bfloat16
    )
    out_sum = jnp.einsum("je,jcd->ecd", owners, back_part, preferred_element_type=jnp.float32)
    dx_sum = jnp.einsum("je,jcd->ecd", owners, back_dx, preferred_element_type=jnp.float32)
    blank = jnp.zeros((1, width), jnp.float32)
    out_vals = jnp.take(jnp.concatenate([out_sum.reshape(-1, width), blank]), slot, axis=0)
    dx_vals = jnp.take(jnp.concatenate([dx_sum.reshape(-1, width), blank]), slot, axis=0)
    mixed = jnp.sum(out_vals.reshape(count, topk, width) * gates[:, :, None], axis=1).astype(
        jnp.bfloat16
    )
    token_grad = jnp.sum(dx_vals.reshape(count, topk, width), axis=1).astype(jnp.bfloat16)
    return (
        mixed,
        token_grad,
        new_w_in[None],
        new_w_out[None],
        new_m_in[None],
        new_v_in[None],
        new_m_out[None],
        new_v_out[None],
    )


def solution(mesh):
    in_specs = (
        P(("dp", "expert"), None),
        P(("dp", "expert"), None),
        P(("dp", "expert"), None),
        P(("dp", "expert"), None),
        P(),
        P(),
        P(),
        P("expert", None, None),
        P("expert", None, None),
        P("expert", None, None),
        P("expert", None, None),
        P("expert", None, None),
        P("expert", None, None),
    )
    out_specs = (
        P(("dp", "expert"), None),
        P(("dp", "expert"), None),
        P("expert", None, None),
        P("expert", None, None),
        P("expert", None, None),
        P("expert", None, None),
        P("expert", None, None),
        P("expert", None, None),
    )
    return jax.shard_map(local, mesh=mesh, in_specs=in_specs, out_specs=out_specs, check_vma=False)
```

profile of v0, /device:TPU:1, one launch (start us, length us, event | category | flops | bytes accessed | tf_op | source)
XLA Modules:
  0.0 611.7 jit_solution(7909800098683608369)
XLA Ops:
  22.8 4.2 scatter_custom_fusion
  35.7 8.4 %broadcast_select_fusion = (bf16[64,24,2048]{2,1,0:T(8,128)(2,1)}, bf16[64,24,2048]{2,1,0:T(8,128)(2,1)S(1)}) fusion(bf16[64,24,2048]{2,1,0:T(8,128)(2,1)} %gather_fusion.3, pred[64]{0:T(512)(128)(4,1)S(1)} %get-tuple-element.27, bf16[64,24,2048]{2,1,0:T(8,128)(2,1)} %gather_fusion.1), kind=kLoop, calls=%fused_computation.13 | loop fusion | flops 6291456 | bytes 25165888 | tf_op jit(solution)/shard_map/jit(_take)/select_n | solution.py:110
  44.1 84.6 %all_to_all.20 = bf16[64,24,2048]{2,1,0:T(8,128)(2,1)} all-to-all(bf16[64,24,2048]{2,1,0:T(8,128)(2,1)S(1)} %get-tuple-element.38), channel_id=1, replica_groups=mesh['dp'=2,'expert'=64] {'expert'}, dimensions={0} | all-to-all | bytes 12582912 | tf_op jit(solution)/shard_map/all_to_all | solution.py:112
  128.6 6.5 %all-to-all-start.2 = ((bf16[64,24,2048]{2,1,0:T(8,128)(2,1)}), bf16[64,24,2048]{2,1,0:T(8,128)(2,1)}, u32[]{:S(2)}, u32[]{:S(2)}) async-start(bf16[64,24,2048]{2,1,0:T(8,128)(2,1)} %get-tuple-element.37), calls=%async_computation.2 | async-start | bytes 12582912 | tf_op jit(solution)/shard_map/all_to_all | solution.py:113
  138.9 74.9 %collective-permute-done = bf16[1024,256]{1,0:T(8,128)(2,1)} collective-permute-done((bf16[1024,256]{1,0:T(8,128)(2,1)S(1)}, bf16[1024,256]{1,0:T(8,128)(2,1)}, u32[]{:S(2)}, u32[]{:S(2)}) %collective-permute-start) | collective-permute-done | bytes 524320 | tf_op jit(solution)/shard_map/ppermute | solution.py:17
  215.4 7.1 %collective-permute-done.1 = bf16[1024,256]{1,0:T(8,128)(2,1)S(1)} collective-permute-done((bf16[1024,256]{1,0:T(8,128)(2,1)}, bf16[1024,256]{1,0:T(8,128)(2,1)S(1)}, u32[]{:S(2)}, u32[]{:S(2)}) %collective-permute-start.1) | collective-permute-done | bytes 524320 | tf_op jit(solution)/shard_map/ppermute | solution.py:17
  223.4 4.9 collective-permute-done.2
  229.2 7.6 %collective-permute-done.3 = bf16[128,2048]{1,0:T(8,128)(2,1)S(1)} collective-permute-done((bf16[128,2048]{1,0:T(8,128)(2,1)}, bf16[128,2048]{1,0:T(8,128)(2,1)S(1)}, u32[]{:S(2)}, u32[]{:S(2)}) %collective-permute-start.3) | collective-permute-done | bytes 524320 | tf_op jit(solution)/shard_map/ppermute | solution.py:17
  245.1 12.8 %all-gather.9.cloned.1.call-done = bf16[256,2048]{1,0:T(8,128)(2,1)} async-done(((bf16[128,2048]{1,0:T(8,128)(2,1)}), bf16[256,2048]{1,0:T(8,128)(2,1)}) %all-gather.9.cloned.1.call-update) | async-done | bytes 1048592 | tf_op jit(solution)/shard_map/all_gather | solution.py:31
  259.5 5.7 fusion.37
  265.3 6.0 fusion.12
  271.3 4.5 convolution_convert_fusion
  275.8 10.3 %all-to-all-start.3 = ((bf16[64,24,2048]{2,1,0:T(8,128)(2,1)}), bf16[64,24,2048]{2,1,0:T(8,128)(2,1)}, u32[]{:S(2)}, u32[]{:S(2)}) async-start(bf16[64,24,2048]{2,1,0:T(8,128)(2,1)} %bitcast.95), calls=%async_computation.3 | async-start | bytes 12582912 | tf_op jit(solution)/shard_map/all_to_all | solution.py:140
  289.7 75.4 %collective-permute-done.8 = bf16[128,2048]{1,0:T(8,128)(2,1)S(1)} collective-permute-done((bf16[128,2048]{1,0:T(8,128)(2,1)S(1)}, bf16[128,2048]{1,0:T(8,128)(2,1)S(1)}, u32[]{:S(2)}, u32[]{:S(2)}) %collective-permute-start.8) | collective-permute-done | bytes 524320 | tf_op jit(solution)/shard_map/ppermute | solution.py:17
  373.6 5.5 collective-permute-done.10
  381.5 6.4 %collective-permute-done.11 = bf16[128,2048]{1,0:T(8,128)(2,1)} collective-permute-done((bf16[128,2048]{1,0:T(8,128)(2,1)}, bf16[128,2048]{1,0:T(8,128)(2,1)}, u32[]{:S(2)}, u32[]{:S(2)}) %collective-permute-start.11) | collective-permute-done | bytes 524320 | tf_op jit(solution)/shard_map/ppermute | solution.py:17
  388.4 7.0 %fusion.36 = f32[256,2048]{1,0:T(8,128)} fusion(bf16[1536,2048]{1,0:T(8,128)(2,1)} %bitcast.14, f32[1536,256]{1,0:T(8,128)} %fusion.37), kind=kOutput, calls=%fused_computation.94 | convolution fusion | flops 1614151680 | bytes 9961472 | tf_op jit(solution)/shard_map/dot_general | solution.py:133
  395.4 6.0 fusion.38
  401.5 6.0 convolution_convert_fusion.1
  407.5 15.6 %all-to-all-start.1 = ((bf16[64,24,2048]{2,1,0:T(8,128)(2,1)}), bf16[64,24,2048]{2,1,0:T(8,128)(2,1)}, u32[]{:S(2)}, u32[]{:S(2)}) async-start(bf16[64,24,2048]{2,1,0:T(8,128)(2,1)} %bitcast.94), calls=%async_computation.1 | async-start | bytes 12582912 | tf_op jit(solution)/shard_map/all_to_all | solution.py:137
  425.6 74.8 %collective-permute-done.4 = bf16[1024,256]{1,0:T(8,128)(2,1)S(1)} collective-permute-done((bf16[1024,256]{1,0:T(8,128)(2,1)S(1)}, bf16[1024,256]{1,0:T(8,128)(2,1)S(1)}, u32[]{:S(2)}, u32[]{:S(2)}) %collective-permute-start.4) | collective-permute-done | bytes 524320 | tf_op jit(solution)/shard_map/ppermute | solution.py:17
  503.5 5.3 collective-permute-done.5
  509.6 4.9 collective-permute-done.6
  515.8 7.0 %collective-permute-done.7 = bf16[1024,256]{1,0:T(8,128)(2,1)S(1)} collective-permute-done((bf16[1024,256]{1,0:T(8,128)(2,1)}, bf16[1024,256]{1,0:T(8,128)(2,1)S(1)}, u32[]{:S(2)}, u32[]{:S(2)}) %collective-permute-start.7) | collective-permute-done | bytes 524320 | tf_op jit(solution)/shard_map/ppermute | solution.py:17
  523.8 7.8 %fusion.20 = (bf16[1,256,2048]{2,1,0:T(8,128)(2,1)}, f32[1,256,2048]{2,1,0:T(8,128)}, bf16[1,256,2048]{2,1,0:T(8,128)(2,1)}) fusion(f32[256,2048]{1,0:T(8,128)} %get-tuple-element.24, bf16[256,2048]{1,0:T(8,128)(2,1)} %all-gather.17.cloned.1.call-done, bf16[1,256,2048]{2,1,0:T(8,128)(2,1)} %param.29, pred[]{:T(512)S(6)} %ne.24, ...), kind=kLoop, calls=%fused_computation.44 | loop fusion | flops 12058624 | bytes 13631489 | tf_op jit(solution)/shard_map/broadcast_in_dim | solution.py:167
  531.6 13.2 %all-gather.13.cloned.1.call-done = bf16[2048,256]{1,0:T(8,128)(2,1)} async-done(((bf16[1024,256]{1,0:T(8,128)(2,1)}), bf16[2048,256]{1,0:T(8,128)(2,1)}) %all-gather.13.cloned.1.call-update) | async-done | bytes 1048592 | tf_op jit(solution)/shard_map/all_gather | solution.py:31
  544.8 8.1 %fusion.19 = (bf16[1,2048,256]{2,1,0:T(8,128)(2,1)}, f32[1,2048,256]{2,1,0:T(8,128)}, bf16[1,2048,256]{2,1,0:T(8,128)(2,1)}) fusion(f32[2048,256]{1,0:T(8,128)} %get-tuple-element.23, bf16[2048,256]{1,0:T(8,128)(2,1)} %all-gather.13.cloned.1.call-done, bf16[1,2048,256]{2,1,0:T(8,128)(2,1)} %param.27, pred[]{:T(512)S(6)} %ne.24, ...), kind=kLoop, calls=%fused_computation.43 | loop fusion | flops 12058624 | bytes 13631489 | tf_op jit(solution)/shard_map/broadcast_in_dim | solution.py:165
  552.9 9.7 %fusion = f32[16,24,2048]{2,0,1:T(8,128)S(1)} fusion(bf16[64,24,2048]{2,1,0:T(8,128)(2,1)} %all-to-all-done.3, s32[64]{0:T(128)S(1)} %get-tuple-element.28), kind=kOutput, calls=%fused_computation.9 | convolution fusion | flops 100664320 | bytes 9437440 | tf_op jit(solution)/shard_map/je,jcd->ecd/dot_general | solution.py:151
  564.4 9.5 %fusion.2 = f32[16,24,2048]{2,0,1:T(8,128)S(1)} fusion(bf16[64,24,2048]{2,1,0:T(8,128)(2,1)} %all-to-all-done.1, s32[64]{0:T(128)S(1)} %get-tuple-element.28), kind=kOutput, calls=%fused_computation.11 | convolution fusion | flops 100664320 | bytes 9437440 | tf_op jit(solution)/shard_map/je,jcd->ecd/dot_general | solution.py:150
  578.3 5.5 gather_fusion.4
  586.5 5.0 broadcast_select_fusion.2
  594.0 4.0 multiply_reduce_fusion
  (119 shorter events, 82.0 us)
Async XLA Ops:
  7.2 12.9 %copy-start = (s32[64]{0:T(128)S(1)}, s32[64]{0:T(128)}, u32[]{:S(2)}) copy-start(s32[64]{0:T(128)} %param.22) | copy-start | bytes 772
  13.0 2.5 copy-start.16
  22.8 5.7 slice-start
  128.6 85.4 %copy-start.3 = (f32[1,256,2048]{2,1,0:T(8,128)S(1)}, f32[1,256,2048]{2,1,0:T(8,128)}, u32[]{:S(2)}) copy-start(f32[1,256,2048]{2,1,0:T(8,128)} %param.25) | copy-start | bytes 6291460
  128.6 136.7 %all-to-all-start.2 = ((bf16[64,24,2048]{2,1,0:T(8,128)(2,1)}), bf16[64,24,2048]{2,1,0:T(8,128)(2,1)}, u32[]{:S(2)}, u32[]{:S(2)}) async-start(bf16[64,24,2048]{2,1,0:T(8,128)(2,1)} %get-tuple-element.37), calls=%async_computation.2 | async-start | bytes 12582912 | tf_op jit(solution)/shard_map/all_to_all | solution.py:113
  135.1 106.9 %all-gather.7.cloned.1.call-start = ((), (), s32[]{:S(2)}) async-start(), calls=%async_computation.4 | async-start | bytes 1572864 | tf_op jit(solution)/shard_map/all_gather | solution.py:31
  136.4 77.4 %collective-permute-start = (bf16[1024,256]{1,0:T(8,128)(2,1)S(1)}, bf16[1024,256]{1,0:T(8,128)(2,1)}, u32[]{:S(2)}, u32[]{:S(2)}) collective-permute-start(bf16[1024,256]{1,0:T(8,128)(2,1)S(1)} %dynamic-slice_convert_fusion.1), channel_id=1, source_target_pairs={{0,16},{1,17},{2,18},{3,19},{4,20},{5,21},{6,22},{7,23},{8,24},{9,... | collective-permute-start | bytes 1572872 | tf_op jit(solution)/shard_map/ppermute | solution.py:17
  213.8 8.7 %collective-permute-start.1 = (bf16[1024,256]{1,0:T(8,128)(2,1)}, bf16[1024,256]{1,0:T(8,128)(2,1)S(1)}, u32[]{:S(2)}, u32[]{:S(2)}) collective-permute-start(bf16[1024,256]{1,0:T(8,128)(2,1)} %collective-permute-done), channel_id=1, source_target_pairs={{0,16},{1,17},{2,18},{3,19},{4,20},{5,21},{6,22},{7,23},{8,24},{9,... | collective-permute-start | bytes 1572872 | tf_op jit(solution)/shard_map/ppermute | solution.py:17
  214.1 14.2 %collective-permute-start.2 = (bf16[128,2048]{1,0:T(8,128)(2,1)S(1)}, bf16[128,2048]{1,0:T(8,128)(2,1)}, u32[]{:S(2)}, u32[]{:S(2)}) collective-permute-start(bf16[128,2048]{1,0:T(8,128)(2,1)S(1)} %dynamic-slice_convert_fusion), channel_id=1, source_target_pairs={{0,16},{1,17},{2,18},{3,19},{4,20},{5,21},{6,22},{7,23},{8,24},{9,... | collective-permute-start | bytes 1572872 | tf_op jit(solution)/shard_map/ppermute | solution.py:17
  223.3 34.5 %all-gather.9.cloned.1.call-start = ((), (), s32[]{:S(2)}) async-start(), calls=%async_computation.5 | async-start | bytes 1572864 | tf_op jit(solution)/shard_map/all_gather | solution.py:31
  228.3 8.5 %collective-permute-start.3 = (bf16[128,2048]{1,0:T(8,128)(2,1)}, bf16[128,2048]{1,0:T(8,128)(2,1)S(1)}, u32[]{:S(2)}, u32[]{:S(2)}) collective-permute-start(bf16[128,2048]{1,0:T(8,128)(2,1)} %collective-permute-done.2), channel_id=1, source_target_pairs={{0,16},{1,17},{2,18},{3,19},{4,20},{5,21},{6,22},{7,23},{8,24},{9,... | collective-permute-start | bytes 1572872 | tf_op jit(solution)/shard_map/ppermute | solution.py:17
  265.3 6.0 copy-start.5
  271.3 4.5 copy-start.8
  275.8 131.7 %all-to-all-start.3 = ((bf16[64,24,2048]{2,1,0:T(8,128)(2,1)}), bf16[64,24,2048]{2,1,0:T(8,128)(2,1)}, u32[]{:S(2)}, u32[]{:S(2)}) async-start(bf16[64,24,2048]{2,1,0:T(8,128)(2,1)} %bitcast.95), calls=%async_computation.3 | async-start | bytes 12582912 | tf_op jit(solution)/shard_map/all_to_all | solution.py:140
  286.1 237.6 %all-gather.15.cloned.1.call-start = ((), (), s32[]{:S(2)}) async-start(), calls=%async_computation.8 | async-start | bytes 1572864 | tf_op jit(solution)/shard_map/all_gather | solution.py:31
  287.3 77.8 %collective-permute-start.8 = (bf16[128,2048]{1,0:T(8,128)(2,1)S(1)}, bf16[128,2048]{1,0:T(8,128)(2,1)S(1)}, u32[]{:S(2)}, u32[]{:S(2)}) collective-permute-start(bf16[128,2048]{1,0:T(8,128)(2,1)S(1)} %dynamic-slice_bitcast_fusion.1), channel_id=1, source_target_pairs={{0,16},{1,17},{2,18},{3,19},{4,20},{5,21},{6,22},{7,23},{8,24},{9,... | collective-permute-start | bytes 1572872 | tf_op jit(solution)/shard_map/ppermute | solution.py:17
  365.1 8.4 %collective-permute-start.9 = (bf16[128,2048]{1,0:T(8,128)(2,1)S(1)}, bf16[128,2048]{1,0:T(8,128)(2,1)}, u32[]{:S(2)}, u32[]{:S(2)}) collective-permute-start(bf16[128,2048]{1,0:T(8,128)(2,1)S(1)} %collective-permute-done.8), channel_id=1, source_target_pairs={{0,16},{1,17},{2,18},{3,19},{4,20},{5,21},{6,22},{7,23},{8,24},{9,... | collective-permute-start | bytes 1572872 | tf_op jit(solution)/shard_map/ppermute | solution.py:17
  368.4 10.7 %collective-permute-start.10 = (bf16[128,2048]{1,0:T(8,128)(2,1)}, bf16[128,2048]{1,0:T(8,128)(2,1)}, u32[]{:S(2)}, u32[]{:S(2)}) collective-permute-start(bf16[128,2048]{1,0:T(8,128)(2,1)} %dynamic-slice_bitcast_fusion), channel_id=1, source_target_pairs={{0,16},{1,17},{2,18},{3,19},{4,20},{5,21},{6,22},{7,23},{8,24},{9,... | collective-permute-start | bytes 1572872 | tf_op jit(solution)/shard_map/ppermute | solution.py:17
  373.5 150.2 %all-gather.17.cloned.1.call-start = ((), (), s32[]{:S(2)}) async-start(), calls=%async_computation.9 | async-start | bytes 1572864 | tf_op jit(solution)/shard_map/all_gather | solution.py:31
  379.1 8.8 %collective-permute-start.11 = (bf16[128,2048]{1,0:T(8,128)(2,1)}, bf16[128,2048]{1,0:T(8,128)(2,1)}, u32[]{:S(2)}, u32[]{:S(2)}) collective-permute-start(bf16[128,2048]{1,0:T(8,128)(2,1)} %collective-permute-done.10), channel_id=1, source_target_pairs={{0,16},{1,17},{2,18},{3,19},{4,20},{5,21},{6,22},{7,23},{8,24},{9,... | collective-permute-start | bytes 1572872 | tf_op jit(solution)/shard_map/ppermute | solution.py:17
  388.0 135.8 %all-reduce.5.cloned.1.call-start = ((), (), s32[]{:S(2)}) async-start(), calls=%async_computation.10 | async-start | bytes 8388608 | tf_op jit(solution)/shard_map/psum | solution.py:144
  388.4 7.0 %copy-start.9 = (bf16[1536,256]{1,0:T(8,128)(2,1)S(1)}, bf16[1536,256]{1,0:T(8,128)(2,1)}, u32[]{:S(2)}) copy-start(bf16[1536,256]{1,0:T(8,128)(2,1)} %copy-done.8) | copy-start | bytes 2359300
  407.5 15.6 %copy-start.7 = (bf16[1,2048,256]{2,1,0:T(8,128)(2,1)S(1)}, bf16[1,2048,256]{2,1,0:T(8,128)(2,1)}, u32[]{:S(2)}) copy-start(bf16[1,2048,256]{2,1,0:T(8,128)(2,1)} %param.26) | copy-start | bytes 3145732
  407.5 157.0 %all-to-all-start.1 = ((bf16[64,24,2048]{2,1,0:T(8,128)(2,1)}), bf16[64,24,2048]{2,1,0:T(8,128)(2,1)}, u32[]{:S(2)}, u32[]{:S(2)}) async-start(bf16[64,24,2048]{2,1,0:T(8,128)(2,1)} %bitcast.94), calls=%async_computation.1 | async-start | bytes 12582912 | tf_op jit(solution)/shard_map/all_to_all | solution.py:137
  423.1 108.5 %all-gather.11.cloned.1.call-start = ((), (), s32[]{:S(2)}) async-start(), calls=%async_computation.6 | async-start | bytes 1572864 | tf_op jit(solution)/shard_map/all_gather | solution.py:31
  423.2 77.2 %collective-permute-start.4 = (bf16[1024,256]{1,0:T(8,128)(2,1)S(1)}, bf16[1024,256]{1,0:T(8,128)(2,1)S(1)}, u32[]{:S(2)}, u32[]{:S(2)}) collective-permute-start(bf16[1024,256]{1,0:T(8,128)(2,1)S(1)} %dynamic-slice_bitcast_fusion.3), channel_id=1, source_target_pairs={{0,16},{1,17},{2,18},{3,19},{4,20},{5,21},{6,22},{7,23},{8,24},{9,... | collective-permute-start | bytes 1572872 | tf_op jit(solution)/shard_map/ppermute | solution.py:17
  500.4 8.3 %collective-permute-start.5 = (bf16[1024,256]{1,0:T(8,128)(2,1)S(1)}, bf16[1024,256]{1,0:T(8,128)(2,1)S(1)}, u32[]{:S(2)}, u32[]{:S(2)}) collective-permute-start(bf16[1024,256]{1,0:T(8,128)(2,1)S(1)} %collective-permute-done.4), channel_id=1, source_target_pairs={{0,16},{1,17},{2,18},{3,19},{4,20},{5,21},{6,22},{7,23},{8,24},{9,... | collective-permute-start | bytes 1572872 | tf_op jit(solution)/shard_map/ppermute | solution.py:17
  501.8 12.6 %collective-permute-start.6 = (bf16[1024,256]{1,0:T(8,128)(2,1)S(1)}, bf16[1024,256]{1,0:T(8,128)(2,1)}, u32[]{:S(2)}, u32[]{:S(2)}) collective-permute-start(bf16[1024,256]{1,0:T(8,128)(2,1)S(1)} %dynamic-slice_bitcast_fusion.2), channel_id=1, source_target_pairs={{0,16},{1,17},{2,18},{3,19},{4,20},{5,21},{6,22},{7,23},{8,24},{9,... | collective-permute-start | bytes 1572872 | tf_op jit(solution)/shard_map/ppermute | solution.py:17
  509.5 35.2 %all-gather.13.cloned.1.call-start = ((), (), s32[]{:S(2)}) async-start(), calls=%async_computation.7 | async-start | bytes 1572864 | tf_op jit(solution)/shard_map/all_gather | solution.py:31
  514.4 8.4 %collective-permute-start.7 = (bf16[1024,256]{1,0:T(8,128)(2,1)}, bf16[1024,256]{1,0:T(8,128)(2,1)S(1)}, u32[]{:S(2)}, u32[]{:S(2)}) collective-permute-start(bf16[1024,256]{1,0:T(8,128)(2,1)} %collective-permute-done.6), channel_id=1, source_target_pairs={{0,16},{1,17},{2,18},{3,19},{4,20},{5,21},{6,22},{7,23},{8,24},{9,... | collective-permute-start | bytes 1572872 | tf_op jit(solution)/shard_map/ppermute | solution.py:17
  523.8 21.0 %copy-start.6 = (bf16[2048,256]{1,0:T(8,128)(2,1)S(1)}, bf16[2048,256]{1,0:T(8,128)(2,1)}, u32[]{:S(2)}) copy-start(bf16[2048,256]{1,0:T(8,128)(2,1)} %all-gather.7.cloned.1.call-done) | copy-start | bytes 3145732
  598.0 6.4 %copy-start.1 = (s32[64]{0:T(128)S(1)}, s32[64]{0:T(128)}, u32[]{:S(2)}) copy-start(s32[64]{0:T(128)} %param.22) | copy-start | bytes 772
  (8 other events, 9.2 us)
Sparse Core Ops, SparseCore 0:
  223.5 18.4 all-gather.6
  244.2 13.6 all-gather.8
  373.7 18.5 all-gather.14
  393.8 14.0 all-gather.16
  411.0 35.2 all-reduce.4
  509.7 19.7 all-gather.10
  531.7 13.0 all-gather.12
where the time goes:
time: 621 us; the launch traced here: 612 us
  waiting for transfers between devices  306 us (49%)
  blocking collectives  84.6 us (14%)
  matrix products  54.4 us (9%)
  starting transfers between devices  51.9 us (8%)
  local copies, waits for them, and re-layouts  51.8 us (8%)
  other arithmetic  47.1 us (8%)
  between operations  15.6 us (3%)
    ppermute x12, waiting for transfers between devices, relay(): return lax.ppermute(block, ('dp', 'expert'), route)  277 us
    all_to_all x1, blocking collectives, local(): lax.all_to_all(send_x, 'expert', split_axis=0, concat_axis=0, tiled=True)  84.6 us
    all_gather x6, waiting for transfers between devices, migrate(): return tuple((lax.all_gather(m, 'dp', axis=0, tiled=True) for m in moved))  29.1 us
    ppermute x12, starting transfers between devices, relay(): return lax.ppermute(block, ('dp', 'expert'), route)  18.9 us
    all_to_all x1, starting transfers between devices, local(): lax.all_to_all(part.reshape(nexp, slots, width), 'expert', split_axis=0,...  15.6 us
  transfers between devices with their start and end apart: 22, of which 15 were waited for; matrix products, arithmetic and copies ran while one was open for 10% of the time, Pallas kernels for 0%

commit v1 on v0

--- a/solution.py
+++ b/solution.py
@@ -28,7 +28,14 @@
         )
     )
     moved = relay(relay(halves, step), step)
-    return tuple((lax.all_gather(m, "dp", axis=0, tiled=True) for m in moved))
+    return tuple(
+        (
+            jnp.concatenate(
+                lax.all_to_all(jnp.stack([m] * lax.axis_size("dp")), "dp", 0, 0), axis=0
+            )
+            for m in moved
+        )
+    )
 
 
 def gelu_tanh(value):

time: 621 us -> 584 us (0.940)
  the two profiles are of different devices: /device:TPU:1 before, /device:TPU:76 now
where the time goes in v1:
time: 584 us; the launch traced here: 574 us
  waiting for transfers between devices  245 us (42%)
  blocking collectives  98.2 us (17%)
  starting transfers between devices  67.1 us (11%)
  local copies, waits for them, and re-layouts  51.2 us (9%)
  other arithmetic  50 us (9%)
  matrix products  46.8 us (8%)
  between operations  15.6 us (3%)
    all_to_all x1, blocking collectives, local(): lax.all_to_all(send_x, 'expert', split_axis=0, concat_axis=0, tiled=True)  81.7 us
    all_to_all x1, waiting for transfers between devices, local(): lax.all_to_all(part.reshape(nexp, slots, width), 'expert', split_axis=0,...  75.2 us
    all_to_all x1, waiting for transfers between devices, local(): lax.all_to_all(send_g, 'expert', split_axis=0, concat_axis=0, tiled=True)  73.6 us
    all_to_all x1, waiting for transfers between devices, local(): lax.all_to_all(xpart.reshape(nexp, slots, width), 'expert', split_axis=0,...  70 us
    ppermute x12, waiting for transfers between devices, relay(): return lax.ppermute(block, ('dp', 'expert'), route)  24.3 us
    ppermute x12, starting transfers between devices, relay(): return lax.ppermute(block, ('dp', 'expert'), route)  17.6 us
    all_to_all x3, blocking collectives, migrate(): lax.all_to_all(jnp.stack([m] * lax.axis_size('dp')), 'dp', 0, 0)  16.5 us
    all_to_all x1, starting transfers between devices, local(): lax.all_to_all(xpart.reshape(nexp, slots, width), 'expert', split_axis=0,...  14.3 us
  transfers between devices with their start and end apart: 19, of which 12 were waited for; matrix products, arithmetic and copies ran while one was open for 15% of the time, Pallas kernels for 0%

profile of v1, /device:TPU:76, one launch (start us, length us, event | category | flops | bytes accessed | tf_op | source)
XLA Modules:
  0.0 574.1 jit_solution(18038934507606744217)
XLA Ops:
  19.7 3.7 scatter_custom_fusion.1
  26.8 4.1 scatter_custom_fusion
  42.3 10.6 %broadcast_select_fusion = (bf16[64,24,2048]{2,1,0:T(8,128)(2,1)}, bf16[64,24,2048]{2,1,0:T(8,128)(2,1)}) fusion(bf16[64,24,2048]{2,1,0:T(8,128)(2,1)} %gather_fusion.3, pred[64]{0:T(512)(128)(4,1)S(1)} %get-tuple-element.31, bf16[64,24,2048]{2,1,0:T(8,128)(2,1)} %gather_fusion.1), kind=kLoop, calls=%fused_computation.13 | loop fusion | flops 6291456 | bytes 25165888 | tf_op jit(solution)/shard_map/jit(_take)/select_n | solution.py:117
  59.7 4.6 all_to_all.50
  64.3 81.7 %all_to_all.51 = bf16[64,24,2048]{2,1,0:T(8,128)(2,1)} all-to-all(bf16[64,24,2048]{2,1,0:T(8,128)(2,1)} %get-tuple-element.40), channel_id=1, replica_groups=mesh['dp'=2,'expert'=64] {'expert'}, dimensions={0} | all-to-all | bytes 12582912 | tf_op jit(solution)/shard_map/all_to_all | solution.py:119
  145.9 9.8 %all-to-all-start.4 = ((bf16[64,24,2048]{2,1,0:T(8,128)(2,1)}), bf16[64,24,2048]{2,1,0:T(8,128)(2,1)}, u32[]{:S(2)}, u32[]{:S(2)}) async-start(bf16[64,24,2048]{2,1,0:T(8,128)(2,1)} %get-tuple-element.39), calls=%async_computation.4 | async-start | bytes 12582912 | tf_op jit(solution)/shard_map/all_to_all | solution.py:120
  163.8 73.6 %all-to-all-done.4 = bf16[64,24,2048]{2,1,0:T(8,128)(2,1)} async-done(((bf16[64,24,2048]{2,1,0:T(8,128)(2,1)}), bf16[64,24,2048]{2,1,0:T(8,128)(2,1)}, u32[]{:S(2)}, u32[]{:S(2)}) %all-to-all-start.4) | async-done | bytes 6291488 | tf_op jit(solution)/shard_map/all_to_all | solution.py:120
  237.5 6.6 %fusion.40 = f32[256,2048]{1,0:T(8,128)} fusion(bf16[1536,2048]{1,0:T(8,128)(2,1)} %bitcast.19, f32[1536,256]{1,0:T(8,128)} %fusion.41), kind=kOutput, calls=%fused_computation.106 | convolution fusion | flops 1614151680 | bytes 9961472 | tf_op jit(solution)/shard_map/dot_general | solution.py:140
  244.1 5.6 fusion.14
  256.4 4.5 collective-permute-start.6
  266.5 3.7 collective-permute-done.6
  272.1 3.7 collective-permute-done.8
  277.7 3.7 collective-permute-done.10
  283.3 3.6 collective-permute-done.5
  288.0 4.6 all-to-all-start.6
  306.1 6.6 %all_to_all.52 = bf16[2,1024,256]{2,1,0:T(8,128)(2,1)} all-to-all(bf16[2,1024,256]{2,1,0:T(8,128)(2,1)} %pad_maximum_fusion.3), channel_id=1, replica_groups=mesh['dp'=2,'expert'=64] {'dp'}, dimensions={0} | all-to-all | bytes 2097152 | tf_op jit(solution)/shard_map/all_to_all | solution.py:34
  312.7 4.4 all-to-all-start.8
  317.2 5.9 %subtract_bitcast_fusion.1 = (f32[1,2048,256]{2,1,0:T(8,128)}, bf16[2048,256]{1,0:T(8,128)(2,1)S(1)}, bf16[1,2048,256]{2,1,0:T(8,128)(2,1)}, bf16[1,2048,256]{2,1,0:T(8,128)(2,1)}) fusion(f32[2048,256]{1,0:T(8,128)} %get-tuple-element.23, bf16[1,2048,256]{2,1,0:T(8,128)(2,1)} %param.26, bf16[2,1024,256]{2,1,0:T(8,128)(2,1)} %all-to-all-done.6, pred[]{:T(512)S(6)} %ne.24, ...), kind=kLoop, calls=%fused_computation.29 | loop fusion | flops 12582912 | bytes 14680065 | tf_op jit(solution)/shard_map/broadcast_in_dim | solution.py:169
  323.1 4.5 convolution_convert_fusion
  327.6 5.4 all_to_all.53
  332.9 14.3 %all-to-all-start.5 = ((bf16[64,24,2048]{2,1,0:T(8,128)(2,1)}), bf16[64,24,2048]{2,1,0:T(8,128)(2,1)}, u32[]{:S(2)}, u32[]{:S(2)}) async-start(bf16[64,24,2048]{2,1,0:T(8,128)(2,1)} %bitcast.148), calls=%async_computation.5 | async-start | bytes 12582912 | tf_op jit(solution)/shard_map/all_to_all | solution.py:147
  347.2 5.5 subtract_bitcast_fusion
  352.7 4.5 convolution_convert_fusion.1
  357.3 70.0 %all-to-all-done.5 = bf16[64,24,2048]{2,1,0:T(8,128)(2,1)} async-done(((bf16[64,24,2048]{2,1,0:T(8,128)(2,1)}), bf16[64,24,2048]{2,1,0:T(8,128)(2,1)}, u32[]{:S(2)}, u32[]{:S(2)}) %all-to-all-start.5) | async-done | bytes 6291488 | tf_op jit(solution)/shard_map/all_to_all | solution.py:147
  427.3 12.8 %all-to-all-start.3 = ((bf16[64,24,2048]{2,1,0:T(8,128)(2,1)}), bf16[64,24,2048]{2,1,0:T(8,128)(2,1)}, u32[]{:S(2)}, u32[]{:S(2)}) async-start(bf16[64,24,2048]{2,1,0:T(8,128)(2,1)} %bitcast.149), calls=%async_computation.3 | async-start | bytes 12582912 | tf_op jit(solution)/shard_map/all_to_all | solution.py:144
  440.1 9.5 %fusion = f32[16,24,2048]{2,0,1:T(8,128)S(1)} fusion(bf16[64,24,2048]{2,1,0:T(8,128)(2,1)} %all-to-all-done.5, s32[64]{0:T(128)S(1)} %get-tuple-element.32), kind=kOutput, calls=%fused_computation.9 | convolution fusion | flops 100664320 | bytes 9437440 | tf_op jit(solution)/shard_map/je,jcd->ecd/dot_general | solution.py:158
  451.4 75.2 %all-to-all-done.3 = bf16[64,24,2048]{2,1,0:T(8,128)(2,1)} async-done(((bf16[64,24,2048]{2,1,0:T(8,128)(2,1)}), bf16[64,24,2048]{2,1,0:T(8,128)(2,1)}, u32[]{:S(2)}, u32[]{:S(2)}) %all-to-all-start.3) | async-done | bytes 6291488 | tf_op jit(solution)/shard_map/all_to_all | solution.py:144
  526.6 9.7 %fusion.2 = f32[16,24,2048]{2,0,1:T(8,128)S(1)} fusion(bf16[64,24,2048]{2,1,0:T(8,128)(2,1)} %all-to-all-done.3, s32[64]{0:T(128)S(1)} %get-tuple-element.32), kind=kOutput, calls=%fused_computation.11 | convolution fusion | flops 100664320 | bytes 9437440 | tf_op jit(solution)/shard_map/je,jcd->ecd/dot_general | solution.py:157
  540.4 5.5 gather_fusion.4
  548.6 5.0 broadcast_select_fusion.2
  556.4 4.0 multiply_reduce_fusion
  562.9 3.9 reduce_sum.45
  (131 shorter events, 87.6 us)
Async XLA Ops:
  7.2 25.4 %copy-start = (s32[64]{0:T(128)S(1)}, s32[64]{0:T(128)}, u32[]{:S(2)}) copy-start(s32[64]{0:T(128)} %param.22) | copy-start | bytes 772
  7.2 7.1 %copy-start.18 = (s32[128,2]{0,1:T(2,128)S(1)}, s32[128,2]{0,1:T(2,128)}, u32[]{:S(2)}) copy-start(s32[128,2]{0,1:T(2,128)} %param.19) | copy-start | bytes 3076
  7.2 8.6 %copy-start.16 = (bf16[128,2048]{1,0:T(8,128)(2,1)S(1)}, bf16[128,2048]{1,0:T(8,128)(2,1)}, u32[]{:S(2)}) copy-start(bf16[128,2048]{1,0:T(8,128)(2,1)} %param.18) | copy-start | bytes 1572868
  9.3 31.2 %collective-permute-start = (bf16[1024,256]{1,0:T(8,128)(2,1)}, bf16[1024,256]{1,0:T(8,128)(2,1)}, u32[]{:S(2)}, u32[]{:S(2)}) collective-permute-start(bf16[1024,256]{1,0:T(8,128)(2,1)} %dynamic-slice_convert_fusion.1), channel_id=1, source_target_pairs={{0,16},{1,17},{2,18},{3,19},{4,20},{5,21},{6,22},{7,23},{8,24},{9,... | collective-permute-start | bytes 1572872 | tf_op jit(solution)/shard_map/ppermute | solution.py:17
  13.0 27.7 %collective-permute-start.2 = (bf16[128,2048]{1,0:T(8,128)(2,1)}, bf16[128,2048]{1,0:T(8,128)(2,1)}, u32[]{:S(2)}, u32[]{:S(2)}) collective-permute-start(bf16[128,2048]{1,0:T(8,128)(2,1)} %dynamic-slice_convert_fusion), channel_id=1, source_target_pairs={{0,16},{1,17},{2,18},{3,19},{4,20},{5,21},{6,22},{7,23},{8,24},{9,... | collective-permute-start | bytes 1572872 | tf_op jit(solution)/shard_map/ppermute | solution.py:17
  40.5 12.4 %collective-permute-start.1 = (bf16[1024,256]{1,0:T(8,128)(2,1)}, bf16[1024,256]{1,0:T(8,128)(2,1)S(1)}, u32[]{:S(2)}, u32[]{:S(2)}) collective-permute-start(bf16[1024,256]{1,0:T(8,128)(2,1)} %collective-permute-done), channel_id=1, source_target_pairs={{0,16},{1,17},{2,18},{3,19},{4,20},{5,21},{6,22},{7,23},{8,24},{9,... | collective-permute-start | bytes 1572872 | tf_op jit(solution)/shard_map/ppermute | solution.py:17
  40.7 16.8 %collective-permute-start.3 = (bf16[128,2048]{1,0:T(8,128)(2,1)}, bf16[128,2048]{1,0:T(8,128)(2,1)S(1)}, u32[]{:S(2)}, u32[]{:S(2)}) collective-permute-start(bf16[128,2048]{1,0:T(8,128)(2,1)} %collective-permute-done.2), channel_id=1, source_target_pairs={{0,16},{1,17},{2,18},{3,19},{4,20},{5,21},{6,22},{7,23},{8,24},{9,... | collective-permute-start | bytes 1572872 | tf_op jit(solution)/shard_map/ppermute | solution.py:17
  54.0 5.7 all-to-all-start.1
  59.7 86.2 %copy-start.6 = (bf16[2,1024,256]{2,1,0:T(8,128)(2,1)}, bf16[2,1024,256]{2,1,0:T(8,128)(2,1)S(1)}, u32[]{:S(2)}) copy-start(bf16[2,1024,256]{2,1,0:T(8,128)(2,1)S(1)} %all-to-all-done.1) | copy-start | bytes 3145732
  145.9 11.1 %copy-start.3 = (f32[1,2048,256]{2,1,0:T(8,128)S(1)}, f32[1,2048,256]{2,1,0:T(8,128)}, u32[]{:S(2)}) copy-start(f32[1,2048,256]{2,1,0:T(8,128)} %param.24) | copy-start | bytes 6291460
  145.9 91.5 %all-to-all-start.4 = ((bf16[64,24,2048]{2,1,0:T(8,128)(2,1)}), bf16[64,24,2048]{2,1,0:T(8,128)(2,1)}, u32[]{:S(2)}, u32[]{:S(2)}) async-start(bf16[64,24,2048]{2,1,0:T(8,128)(2,1)} %get-tuple-element.39), calls=%async_computation.4 | async-start | bytes 12582912 | tf_op jit(solution)/shard_map/all_to_all | solution.py:120
  155.7 161.5 %all-reduce.5.cloned.1.call-start = ((), (), s32[]{:S(2)}) async-start(), calls=%async_computation.10 | async-start | bytes 8388608 | tf_op jit(solution)/shard_map/psum | solution.py:151
  237.4 6.6 %copy-start.9 = (f32[1536,256]{1,0:T(8,128)S(1)}, f32[1536,256]{1,0:T(8,128)}, u32[]{:S(2)}) copy-start(f32[1536,256]{1,0:T(8,128)} %fusion.41) | copy-start | bytes 4718596
  237.4 6.6 %copy-start.15 = (bf16[256,2048]{1,0:T(8,128)(2,1)S(1)}, bf16[256,2048]{1,0:T(8,128)(2,1)}, u32[]{:S(2)}) copy-start(bf16[256,2048]{1,0:T(8,128)(2,1)} %fusion.25) | copy-start | bytes 3145732
  237.5 13.2 %slice-start.1 = ((s8[6291456]{0:T(1024)(128)(4,1)}), s8[4194304]{0:T(1024)(128)(4,1)S(1)}, s32[]{:S(2)}) async-start(s8[6291456]{0:T(1024)(128)(4,1)} %bitcast.157), calls=%async_computation.12 | async-start | bytes 8388608
  244.1 6.5 %slice-start.2 = ((s8[6291456]{0:T(1024)(128)(4,1)}), s8[2097152]{0:T(1024)(128)(4,1)S(1)}, s32[]{:S(2)}) async-start(s8[6291456]{0:T(1024)(128)(4,1)} %bitcast.157), calls=%async_computation.13 | async-start | bytes 4194304
  254.0 6.9 %copy-start.11 = (bf16[1,256,2048]{2,1,0:T(8,128)(2,1)S(1)}, bf16[1,256,2048]{2,1,0:T(8,128)(2,1)}, u32[]{:S(2)}) copy-start(bf16[1,256,2048]{2,1,0:T(8,128)(2,1)} %param.28) | copy-start | bytes 3145732
  254.0 7.1 %copy-start.12 = (bf16[1,256,2048]{2,1,0:T(8,128)(2,1)S(1)}, bf16[1,256,2048]{2,1,0:T(8,128)(2,1)}, u32[]{:S(2)}) copy-start(bf16[1,256,2048]{2,1,0:T(8,128)(2,1)} %param.29) | copy-start | bytes 3145732
  255.2 9.3 %collective-permute-start.4 = (bf16[1024,256]{1,0:T(8,128)(2,1)S(1)}, bf16[1024,256]{1,0:T(8,128)(2,1)S(1)}, u32[]{:S(2)}, u32[]{:S(2)}) collective-permute-start(bf16[1024,256]{1,0:T(8,128)(2,1)S(1)} %dynamic-slice_bitcast_fusion.3), channel_id=1, source_target_pairs={{0,16},{1,17},{2,18},{3,19},{4,20},{5,21},{6,22},{7,23},{8,24},{9,... | collective-permute-start | bytes 1572872 | tf_op jit(solution)/shard_map/ppermute | solution.py:17
  256.4 13.8 %collective-permute-start.6 = (bf16[1024,256]{1,0:T(8,128)(2,1)S(1)}, bf16[1024,256]{1,0:T(8,128)(2,1)}, u32[]{:S(2)}, u32[]{:S(2)}) collective-permute-start(bf16[1024,256]{1,0:T(8,128)(2,1)S(1)} %dynamic-slice_bitcast_fusion.2), channel_id=1, source_target_pairs={{0,16},{1,17},{2,18},{3,19},{4,20},{5,21},{6,22},{7,23},{8,24},{9,... | collective-permute-start | bytes 1572872 | tf_op jit(solution)/shard_map/ppermute | solution.py:17
  261.0 14.8 %collective-permute-start.8 = (bf16[128,2048]{1,0:T(8,128)(2,1)S(1)}, bf16[128,2048]{1,0:T(8,128)(2,1)}, u32[]{:S(2)}, u32[]{:S(2)}) collective-permute-start(bf16[128,2048]{1,0:T(8,128)(2,1)S(1)} %dynamic-slice_bitcast_fusion.1), channel_id=1, source_target_pairs={{0,16},{1,17},{2,18},{3,19},{4,20},{5,21},{6,22},{7,23},{8,24},{9,... | collective-permute-start | bytes 1572872 | tf_op jit(solution)/shard_map/ppermute | solution.py:17
  261.1 20.3 %collective-permute-start.10 = (bf16[128,2048]{1,0:T(8,128)(2,1)S(1)}, bf16[128,2048]{1,0:T(8,128)(2,1)}, u32[]{:S(2)}, u32[]{:S(2)}) collective-permute-start(bf16[128,2048]{1,0:T(8,128)(2,1)S(1)} %dynamic-slice_bitcast_fusion), channel_id=1, source_target_pairs={{0,16},{1,17},{2,18},{3,19},{4,20},{5,21},{6,22},{7,23},{8,24},{9,... | collective-permute-start | bytes 1572872 | tf_op jit(solution)/shard_map/ppermute | solution.py:17
  264.5 22.5 %collective-permute-start.5 = (bf16[1024,256]{1,0:T(8,128)(2,1)S(1)}, bf16[1024,256]{1,0:T(8,128)(2,1)S(1)}, u32[]{:S(2)}, u32[]{:S(2)}) collective-permute-start(bf16[1024,256]{1,0:T(8,128)(2,1)S(1)} %collective-permute-done.4), channel_id=1, source_target_pairs={{0,16},{1,17},{2,18},{3,19},{4,20},{5,21},{6,22},{7,23},{8,24},{9,... | collective-permute-start | bytes 1572872 | tf_op jit(solution)/shard_map/ppermute | solution.py:17
  270.2 22.5 %collective-permute-start.7 = (bf16[1024,256]{1,0:T(8,128)(2,1)}, bf16[1024,256]{1,0:T(8,128)(2,1)}, u32[]{:S(2)}, u32[]{:S(2)}) collective-permute-start(bf16[1024,256]{1,0:T(8,128)(2,1)} %collective-permute-done.6), channel_id=1, source_target_pairs={{0,16},{1,17},{2,18},{3,19},{4,20},{5,21},{6,22},{7,23},{8,24},{9,... | collective-permute-start | bytes 1572872 | tf_op jit(solution)/shard_map/ppermute | solution.py:17
  275.8 22.5 %collective-permute-start.9 = (bf16[128,2048]{1,0:T(8,128)(2,1)}, bf16[128,2048]{1,0:T(8,128)(2,1)}, u32[]{:S(2)}, u32[]{:S(2)}) collective-permute-start(bf16[128,2048]{1,0:T(8,128)(2,1)} %collective-permute-done.8), channel_id=1, source_target_pairs={{0,16},{1,17},{2,18},{3,19},{4,20},{5,21},{6,22},{7,23},{8,24},{9,... | collective-permute-start | bytes 1572872 | tf_op jit(solution)/shard_map/ppermute | solution.py:17
  281.4 22.5 %collective-permute-start.11 = (bf16[128,2048]{1,0:T(8,128)(2,1)}, bf16[128,2048]{1,0:T(8,128)(2,1)}, u32[]{:S(2)}, u32[]{:S(2)}) collective-permute-start(bf16[128,2048]{1,0:T(8,128)(2,1)} %collective-permute-done.10), channel_id=1, source_target_pairs={{0,16},{1,17},{2,18},{3,19},{4,20},{5,21},{6,22},{7,23},{8,24},{9,... | collective-permute-start | bytes 1572872 | tf_op jit(solution)/shard_map/ppermute | solution.py:17
  288.0 18.2 %all-to-all-start.6 = ((bf16[2,1024,256]{2,1,0:T(8,128)(2,1)}), bf16[2,1024,256]{2,1,0:T(8,128)(2,1)}, u32[]{:S(2)}, u32[]{:S(2)}) async-start(bf16[2,1024,256]{2,1,0:T(8,128)(2,1)} %pad_maximum_fusion.2), calls=%async_computation.6 | async-start | bytes 2097152 | tf_op jit(solution)/shard_map/all_to_all | solution.py:34
  312.7 14.8 %all-to-all-start.8 = ((bf16[2,128,2048]{2,1,0:T(8,128)(2,1)}), bf16[2,128,2048]{2,1,0:T(8,128)(2,1)}, u32[]{:S(2)}, u32[]{:S(2)}) async-start(bf16[2,128,2048]{2,1,0:T(8,128)(2,1)} %pad_maximum_fusion.4), calls=%async_computation.8 | async-start | bytes 2097152 | tf_op jit(solution)/shard_map/all_to_all | solution.py:34
  332.9 14.3 %copy-start.5 = (f32[1,256,2048]{2,1,0:T(8,128)S(1)}, f32[1,256,2048]{2,1,0:T(8,128)}, u32[]{:S(2)}) copy-start(f32[1,256,2048]{2,1,0:T(8,128)} %param.25) | copy-start | bytes 6291460
  332.9 94.4 %all-to-all-start.5 = ((bf16[64,24,2048]{2,1,0:T(8,128)(2,1)}), bf16[64,24,2048]{2,1,0:T(8,128)(2,1)}, u32[]{:S(2)}, u32[]{:S(2)}) async-start(bf16[64,24,2048]{2,1,0:T(8,128)(2,1)} %bitcast.148), calls=%async_computation.5 | async-start | bytes 12582912 | tf_op jit(solution)/shard_map/all_to_all | solution.py:147
  427.3 99.3 %all-to-all-start.3 = ((bf16[64,24,2048]{2,1,0:T(8,128)(2,1)}), bf16[64,24,2048]{2,1,0:T(8,128)(2,1)}, u32[]{:S(2)}, u32[]{:S(2)}) async-start(bf16[64,24,2048]{2,1,0:T(8,128)(2,1)} %bitcast.149), calls=%async_computation.3 | async-start | bytes 12582912 | tf_op jit(solution)/shard_map/all_to_all | solution.py:144
  560.4 6.4 %copy-start.1 = (s32[64]{0:T(128)S(1)}, s32[64]{0:T(128)}, u32[]{:S(2)}) copy-start(s32[64]{0:T(128)} %param.22) | copy-start | bytes 772
  (12 other events, 34.1 us)
Sparse Core Ops, SparseCore 0:
  254.1 38.9 all-reduce.4
